TPU v7x, 512 devices: a whole 4x4x16 slice. The times are simulated.
512 devices in a mesh: dp: 32 (over z, core), cls: 16 (over y, x).
Axes of the slice: x: 4, y: 4, z: 16, core: 2. Of those that a mesh axis runs over, the one named last changes fastest.
Arguments:
- attended: bfloat16 [442368, 1024], P(('dp', 'cls')), may hold values from -6 to 6
- stream: bfloat16 [442368, 1024], P(('dp', 'cls')), may hold values from -6 to 6
- out_proj: bfloat16 [1024, 1024], P('dp'), may hold values from -0.1875 to 0.1875
- norm_gain: float32 [1024], replicated, may hold values from 0.25 to 1.75
- norm_shift: float32 [1024], replicated, may hold values from -0.75 to 0.75
- head_proj: bfloat16 [1024, 512], P('dp'), may hold values from -0.1875 to 0.1875
- class_weight: bfloat16 [16384, 512], P('cls'), may hold values from -6 to 6
- block_ids: int32 [32, 16, 3], P('dp', 'cls'), may hold values from 0 to 7, as said below
- block_count: int32 [32, 16], P('dp', 'cls'), may hold values from 1 to 3, as said below
- labels: int32 [3072], P('dp'), may hold values from 0 to 16383, as said below
Outputs:
- sample_loss: float32 [3072], P(('dp', 'cls'))
- embed_grad: float32 [3072, 512], P(('dp', 'cls'))
- class_grad: float32 [16384, 512], P('cls', 'dp')
Inputs may be any that keep to these rules, and one draw needn't show every extreme that they name: `block_ids`: within one data group and class shard the 3 block numbers are all different. `block_count`: some data group and class shard has all 3 slots live, another just one. `labels`: every image's class lies in a live slot's block of its own data group.
All inputs are finite; a program needn't handle non-finite values.
Results may differ from a plain program's by a relative error of at most 0.0028.
Values may be sent and summed in bfloat16 or wider, within the bound.
A program may use at most 64 MiB of HBM per device.

v0:
```python
import math

import jax
import jax.numpy as jnp
from jax import lax
from jax.sharding import PartitionSpec as P

P_SIZE = 144
BLOCK_ROWS = 128


LOGIT_SCALE = 64.0
ANGLE_MARGIN = 0.5
NORM_EPSILON = 1e-06


def per_device(
    attended,
    stream,
    out_proj,
    norm_gain,
    norm_shift,
    head_proj,
    class_weight,
    block_ids,
    block_count,
    labels,
):
    tok_rows, model_width = attended.shape
    images = tok_rows // P_SIZE
    embed_width = head_proj.shape[1]
    columns = attended
    product = jnp.dot(
        columns,
        lax.all_gather(out_proj, "dp", axis=0, tiled=True),
        preferred_element_type=jnp.float32,
    )
    mixed = stream.astype(jnp.float32) + product
    token_mean = jnp.mean(mixed, axis=1, keepdims=True)
    centred = mixed - token_mean
    variance = jnp.mean(centred * centred, axis=1, keepdims=True)
    normed = norm_gain * centred / jnp.sqrt(variance + NORM_EPSILON) + norm_shift
    pooled = jnp.mean(normed.reshape(images, P_SIZE, model_width), axis=1).astype(jnp.bfloat16)
    columns = pooled
    embedding = jnp.dot(
        columns,
        lax.all_gather(head_proj, "dp", axis=0, tiled=True),
        preferred_element_type=jnp.float32,
    )
    group_embed = lax.all_gather(embedding, "cls", axis=0, tiled=True)
    embed_norm = jnp.sqrt(jnp.sum(group_embed * group_embed, axis=1) + NORM_EPSILON)
    unit_embed = group_embed / embed_norm[:, None]
    shard_index = lax.axis_index("cls")
    own_start = shard_index * images
    slot_ids = block_ids[0, 0]
    live_count = block_count[0, 0]
    slot_total = slot_ids.shape[0]
    blocks_dev = class_weight.shape[0] // BLOCK_ROWS
    cls_dev = blocks_dev * BLOCK_ROWS
    picked = (
        class_weight.reshape(blocks_dev, BLOCK_ROWS, embed_width)[slot_ids]
        .astype(jnp.float32)
        .reshape(-1, embed_width)
    )
    weight_norm = jnp.sqrt(jnp.sum(picked * picked, axis=1) + NORM_EPSILON)
    unit_weight = picked / weight_norm[:, None]
    cosine = jnp.dot(
        unit_embed,
        unit_weight.T,
        precision=lax.Precision.HIGHEST,
        preferred_element_type=jnp.float32,
    )
    slot_range = jnp.arange(slot_total, dtype=jnp.int32)
    row_range = jnp.arange(BLOCK_ROWS, dtype=jnp.int32)
    slot_live = slot_range < live_count
    live_mask = jnp.broadcast_to(slot_live[:, None], (slot_total, BLOCK_ROWS)).reshape(-1)
    local_label = labels - shard_index * cls_dev
    inside = (local_label >= 0) & (local_label < cls_dev)
    label_block = local_label // BLOCK_ROWS
    label_row = local_label % BLOCK_ROWS
    target_mask = (
        (slot_ids[None, :, None] == label_block[:, None, None])
        & (row_range[None, None, :] == label_row[:, None, None])
        & slot_live[None, :, None]
        & inside[:, None, None]
    ).reshape(labels.shape[0], -1)
    target_cos = cosine * math.cos(ANGLE_MARGIN) - jnp.sqrt(1.0 - cosine * cosine) * math.sin(
        ANGLE_MARGIN
    )
    logits = LOGIT_SCALE * jnp.where(target_mask, target_cos, cosine)
    exponent = jnp.where(live_mask[None, :], jnp.exp(logits - LOGIT_SCALE), 0.0)
    denom_part = jnp.sum(exponent, axis=1)
    target_part = jnp.sum(jnp.where(target_mask, logits, 0.0), axis=1)
    denominator, target_logit = lax.psum((denom_part, target_part), "cls")
    target_float = target_mask.astype(jnp.float32)
    cos_grad = LOGIT_SCALE * (exponent / denominator[:, None] - target_float)
    unit_own = lax.dynamic_slice_in_dim(unit_embed, own_start, images, 0)
    norm_own = lax.dynamic_slice_in_dim(embed_norm, own_start, images, 0)
    grad_part = jnp.dot(
        cos_grad, unit_weight, precision=lax.Precision.HIGHEST, preferred_element_type=jnp.float32
    )
    unit_grad = lax.psum_scatter(grad_part, "cls", scatter_dimension=0, tiled=True)
    embed_grad = (
        unit_grad - unit_own * jnp.sum(unit_own * unit_grad, axis=1, keepdims=True)
    ) / norm_own[:, None]
    loss_group = jnp.log(denominator) + LOGIT_SCALE - target_logit
    sample_loss = lax.dynamic_slice_in_dim(loss_group, own_start, images, 0)
    weight_unit_grad = lax.dot_general(
        cos_grad,
        unit_embed,
        (((0,), (0,)), ((), ())),
        precision=lax.Precision.HIGHEST,
        preferred_element_type=jnp.float32,
    )
    weight_grad = (
        weight_unit_grad
        - unit_weight * jnp.sum(unit_weight * weight_unit_grad, axis=1, keepdims=True)
    ) / weight_norm[:, None]
    block_range = jnp.arange(blocks_dev, dtype=jnp.int32)
    placement = ((block_range[:, None] == slot_ids[None, :]) & slot_live[None, :]).astype(
        jnp.float32
    )
    dense_grad = jnp.dot(
        placement,
        weight_grad.reshape(slot_total, -1),
        precision=lax.Precision.HIGHEST,
        preferred_element_type=jnp.float32,
    ).reshape(cls_dev, embed_width)
    class_grad = lax.psum_scatter(dense_grad, "dp", scatter_dimension=1, tiled=True)
    return (sample_loss, embed_grad, class_grad)


def solution(mesh):
    placed = (
        P(("dp", "cls"), None),
        P(("dp", "cls"), None),
        P("dp", None),
        P(),
        P(),
        P("dp", None),
        P("cls", None),
        P("dp", "cls", None),
        P("dp", "cls"),
        P("dp"),
    )
    return jax.shard_map(
        per_device,
        mesh=mesh,
        in_specs=placed,
        out_specs=(P(("dp", "cls")), P(("dp", "cls"), None), P("cls", "dp")),
        check_vma=False,
    )
```

profile of v0, /device:TPU:1, one launch (start us, length us, event | category | flops | bytes accessed | tf_op | source)
XLA Modules:
  0.0 453.8 jit_solution(10540326014448557011)
XLA Ops:
  8.0 0.7 all-gather.6.cloned.1.call-update
  10.7 1.8 gather_fusion
  13.6 0.7 broadcast_compare_fusion
  14.6 72.7 %all-gather.4.cloned.1.call-done = bf16[1024,1024]{1,0:T(8,128)(2,1)} async-done(((bf16[32,1024]{1,0:T(8,128)(2,1)}), bf16[1024,1024]{1,0:T(8,128)(2,1)}) %all-gather.4.cloned.1.call-update) | async-done | bytes 2097168 | tf_op jit(solution)/shard_map/all_gather | solution.py:35
  87.3 4.2 fusion.14
  92.2 2.3 divide_add_fusion
  94.5 2.3 reduce_sum.83
  96.8 60.2 %all-gather.6.cloned.1.call-done = bf16[1024,512]{1,0:T(8,128)(2,1)} async-done(((bf16[32,512]{1,0:T(8,128)(2,1)}), bf16[1024,512]{1,0:T(8,128)(2,1)}) %all-gather.6.cloned.1.call-update) | async-done | bytes 1048592 | tf_op jit(solution)/shard_map/all_gather | solution.py:47
  157.0 1.5 convolution_bitcast_fusion
  158.5 18.6 %all-gather = f32[16,6,512]{2,1,0:T(8,128)S(1)} all-gather(f32[1,6,512]{2,1,0:T(8,128)S(1)} %convolution_bitcast_fusion), channel_id=1, replica_groups=mesh['dp'=32,'cls'=16] {'cls'}, dimensions={0}, use_global_device_ids=true | all-gather | bytes 208896 | tf_op jit(solution)/shard_map/all_gather | solution.py:50
  177.3 1.0 fusion.1
  178.4 31.2 %all-reduce.1 = (f32[96]{0:T(128)S(1)}, f32[96]{0:T(128)S(1)}) all-reduce(f32[96]{0:T(128)S(1)} %get-tuple-element.4, f32[96]{0:T(128)S(1)} %get-tuple-element.3), channel_id=1, replica_groups=mesh['dp'=32,'cls'=16] {'cls'}, use_global_device_ids=true, to_apply=%region_8.9 | all-reduce | flops 192 | bytes 1536 | tf_op jit(solution)/shard_map/psum | solution.py:94
  209.6 1.9 multiply_reduce_fusion.1
  211.4 1.4 fusion.11
  212.8 2.3 subtract_divide_fusion
  215.1 1.7 reshape.161
  216.9 2.5 fusion.4
  219.4 3.3 reshape.162
  222.6 2.9 copy.15
  225.6 1.3 dynamic-slice
  228.2 105.9 %all-reduce.4.cloned.1.call-done = f32[96,512]{1,0:T(8,128)} async-done(((f32[96,512]{1,0:T(8,128)}), f32[96,512]{1,0:T(8,128)}) %all-reduce.4.cloned.1.call-update) | async-done | bytes 196624
  334.1 0.9 multiply_reduce_fusion.4
  335.0 1.4 subtract_divide_fusion.1
  336.4 110.9 %reduce-scatter.2.cloned.1.call-done = f32[1024,16]{0,1:T(8,128)} async-done(((f32[1024,512]{0,1:T(8,128)}), f32[1024,16]{0,1:T(8,128)}) %reduce-scatter.2.cloned.1.call-update) | async-done | bytes 65552 | tf_op jit(solution)/shard_map/reduce_scatter | solution.py:129
  (37 shorter events, 5.1 us)
Async XLA Ops:
  7.2 80.1 %copy-start = (bf16[864,1024]{1,0:T(8,128)(2,1)S(1)}, bf16[864,1024]{1,0:T(8,128)(2,1)}, u32[]{:S(2)}) copy-start(bf16[864,1024]{1,0:T(8,128)(2,1)} %param.10) | copy-start | bytes 5308420
  7.2 80.1 %all-gather.4.cloned.1.call-start = ((), (), s32[]{:S(2)}) async-start(), calls=%async_computation.1 | async-start | bytes 2162688 | tf_op jit(solution)/shard_map/all_gather | solution.py:35
  7.9 149.1 %all-gather.6.cloned.1.call-start = ((), (), s32[]{:S(2)}) async-start(), calls=%async_computation.2 | async-start | bytes 1081344 | tf_op jit(solution)/shard_map/all_gather | solution.py:47
  8.7 325.4 %all-reduce.4.cloned.1.call-start = ((), (), s32[]{:S(2)}) async-start(), calls=%async_computation.4 | async-start | bytes 393216
  91.5 0.7 copy-start.1
  91.5 0.7 copy-start.2
  211.4 5.5 %copy-start.3 = (s32[1,1,3]{2,1,0:T(1,128)S(1)}, s32[1,1,3]{2,1,0:T(1,128)}, u32[]{:S(2)}) copy-start(s32[1,1,3]{2,1,0:T(1,128)} %param.17) | copy-start | bytes 40
  216.8 230.4 %reduce-scatter.2.cloned.1.call-start = ((), (), s32[]{:S(2)}) async-start(), calls=%async_computation.3 | async-start | bytes 2162688 | tf_op jit(solution)/shard_map/reduce_scatter | solution.py:129
Sparse Core Ops, SparseCore 0:
  10.1 77.1 all-gather.3
  89.4 67.6 all-gather.5
  217.0 117.0 all-reduce.3
  337.3 109.9 reduce-scatter.1
where the time goes:
time: 457 us; the launch traced here: 454 us
  waiting for transfers between devices  351 us (77%)
  blocking collectives  49.8 us (11%)
  between operations  15.2 us (3%)
  other arithmetic  13.3 us (3%)
  matrix products  12.4 us (3%)
  local copies, waits for them, and re-layouts  11.9 us (3%)
    reduce_scatter x1, waiting for transfers between devices, per_device(): lax.psum_scatter(dense_grad, 'dp', scatter_dimension=1, tiled=True)  111 us
    unnamed x5, waiting for transfers between devices  107 us
    all_gather x1, waiting for transfers between devices, per_device(): lax.all_gather(out_proj, 'dp', axis=0, tiled=True)  72.7 us
    all_gather x1, waiting for transfers between devices, per_device(): lax.all_gather(head_proj, 'dp', axis=0, tiled=True)  60.2 us
    psum x1, blocking collectives, per_device(): denominator, target_logit = lax.psum((denom_part, target_part), 'cls')  31.2 us
    all_gather x1, blocking collectives, per_device(): group_embed = lax.all_gather(embedding, 'cls', axis=0, tiled=True)  18.6 us
  transfers between devices with their start and end apart: 4, of which 4 were waited for; matrix products, arithmetic and copies ran while one was open for 6% of the time, Pallas kernels for 0%

commit v1 on v0

v1 whole, which is shorter than its diff:
```python
import functools
import math

import jax
import jax.numpy as jnp
from jax import lax
from jax.experimental import pallas as pl
from jax.experimental.pallas import tpu as pltpu
from jax.sharding import PartitionSpec as P

P_SIZE = 144
BLOCK_ROWS = 128
LOGIT_SCALE = 64.0
ANGLE_MARGIN = 0.5
NORM_EPSILON = 1e-06
LANES = 128
PAD = 8

MESH = pl.DeviceIdType.MESH
VMEM = pl.BlockSpec(memory_space=pltpu.VMEM)
HBM = pl.BlockSpec(memory_space=pltpu.HBM)


def remote(src, dst, send, recv, device):
    return pltpu.make_async_remote_copy(
        src_ref=src,
        dst_ref=dst,
        send_sem=send,
        recv_sem=recv,
        device_id=device,
        device_id_type=MESH,
    )


def split(x):
    high = x.astype(jnp.bfloat16)
    low = (x - high.astype(jnp.float32)).astype(jnp.bfloat16)
    return high, low


def dot3(a, b, contract=((1,), (0,))):
    (ah, al), (bh, bl) = a, b
    dims = (contract, ((), ()))
    mul = functools.partial(
        lax.dot_general, dimension_numbers=dims, preferred_element_type=jnp.float32
    )
    return mul(ah, bh) + (mul(ah, bl) + mul(al, bh))


def gather_kernel(chips, op_ref, hp_ref, w_ref, h_ref, ring_s, ring_r, sib_s, sib_r, own_sem):
    dp, cls = lax.axis_index("dp"), lax.axis_index("cls")
    z, core = dp // 2, dp % 2
    right = lax.rem(z + 1, chips) * 2 + core
    left = lax.rem(z + chips - 1, chips) * 2 + core
    sibling = z * 2 + 1 - core
    half = op_ref.shape[0] // 2
    own = []
    for i, (src, dst) in enumerate(((op_ref, w_ref), (hp_ref, h_ref))):
        rows = pl.ds(pl.multiple_of(dp * 2 * half, 2 * half), 2 * half)
        own.append(pltpu.make_async_copy(src, dst.at[rows], own_sem.at[i]))
        own[-1].start()
    barrier = pltpu.get_barrier_semaphore()
    for peer in (left, right, sibling):
        pl.semaphore_signal(barrier, inc=1, device_id=(peer, cls), device_id_type=MESH)
    pl.semaphore_wait(barrier, 3)
    for copy in own:
        copy.wait()

    items = ((w_ref, 0), (w_ref, 1), (h_ref, 0), (h_ref, 1))
    far = chips // 2

    def rows_of(ref, part, chip, k):
        start = pl.multiple_of((chip * 2 + k) * (2 * half) + part * half, half)
        return ref.at[pl.ds(start, half)]

    def ring(item, way, step):
        ref, part = items[item]
        chip = lax.rem(z - (step - 1) + chips, chips) if way == 0 else lax.rem(z + step - 1, chips)
        block = rows_of(ref, part, chip, core)
        peer = right if way == 0 else left
        return remote(
            block, block, ring_s.at[way, step - 1, item], ring_r.at[way, step - 1, item], (peer, cls)
        )

    def arrival(item, way, step):
        ref, part = items[item]
        chip = lax.rem(z - step + chips, chips) if way == 0 else lax.rem(z + step, chips)
        block = rows_of(ref, part, chip, core)
        return remote(
            block,
            block,
            ring_s.at[way, step - 1, item],
            ring_r.at[way, step - 1, item],
            (right if way == 0 else left, cls),
        )

    def goes(item, way, step):
        return step < far or (step == far and items[item][1] == way)

    def hand(item, way, step):
        ref, part = items[item]
        chip = lax.rem(z - step + chips, chips) if way == 0 else lax.rem(z + step, chips)
        block = rows_of(ref, part, chip, core)
        return remote(
            block, block, sib_s.at[way, step, item], sib_r.at[way, step, item], (sibling, cls)
        )

    def taken(item, way, step):
        ref, part = items[item]
        chip = lax.rem(z - step + chips, chips) if way == 0 else lax.rem(z + step, chips)
        block = rows_of(ref, part, chip, 1 - core)
        return remote(
            block, block, sib_s.at[way, step, item], sib_r.at[way, step, item], (sibling, cls)
        )

    sent, handed = [], []
    for item in range(len(items)):
        for way in (0, 1):
            sent.append(ring(item, way, 1))
            sent[-1].start()
        handed.append((item, 0, 0))
        hand(item, 0, 0).start()
    for step in range(1, far + 1):
        for item in range(len(items)):
            for way in (0, 1):
                if not goes(item, way, step):
                    continue
                arrival(item, way, step).wait_recv()
                if goes(item, way, step + 1):
                    sent.append(ring(item, way, step + 1))
                    sent[-1].start()
                handed.append((item, way, step))
                hand(item, way, step).start()
    for key in handed:
        taken(*key).wait_recv()
    for copy in sent:
        copy.wait_send()
    for key in handed:
        hand(*key).wait_send()


def gather(chips, out_proj, head_proj):
    n_dp = 2 * chips
    w_rows, width = out_proj.shape
    h_rows, embed = head_proj.shape
    far = chips // 2
    return pl.pallas_call(
        functools.partial(gather_kernel, chips),
        name="gather_rows",
        out_shape=(
            jax.ShapeDtypeStruct((n_dp * w_rows, width), out_proj.dtype),
            jax.ShapeDtypeStruct((n_dp * h_rows, embed), head_proj.dtype),
        ),
        in_specs=[HBM, HBM],
        out_specs=(VMEM, VMEM),
        scratch_shapes=[
            pltpu.SemaphoreType.DMA((2, far, 4)),
            pltpu.SemaphoreType.DMA((2, far, 4)),
            pltpu.SemaphoreType.DMA((2, far + 1, 4)),
            pltpu.SemaphoreType.DMA((2, far + 1, 4)),
            pltpu.SemaphoreType.DMA((2,)),
        ],
        compiler_params=pltpu.CompilerParams(
            collective_id=0, has_side_effects=True, vmem_limit_bytes=4 << 20
        ),
        cost_estimate=pl.CostEstimate(
            flops=40_000_000_000, bytes_accessed=20 << 20, transcendentals=0
        ),
    )(out_proj, head_proj)


def main_kernel(
    n_dp,
    n_cls,
    images,
    att,
    stream,
    w,
    head,
    weight,
    gain_ref,
    shift_ref,
    slots_ref,
    label_ref,
    loss_ref,
    egrad_ref,
    cgrad_ref,
    mixed,
    pooled_own,
    pooled_all,
    unit_w,
    unit_wt,
    norm_w,
    ids_own,
    ids_all,
    soft_own,
    soft_all,
    eg_own,
    eg_all,
    wg_own,
    wg_all,
    pool_s,
    pool_r,
    ids_s,
    ids_r,
    soft_s,
    soft_r,
    eg_s,
    eg_r,
    wg_s,
    wg_r,
):
    f32 = jnp.float32
    dp, cls = lax.axis_index("dp"), lax.axis_index("cls")
    chips = n_dp // 2
    z, core = dp // 2, dp % 2
    slots = slots_ref.shape[1] - 1
    embed = head.shape[1]
    columns = slots * BLOCK_ROWS
    cls_dev = weight.shape[0]
    blocks_dev = cls_dev // BLOCK_ROWS

    barrier = pltpu.get_barrier_semaphore()
    for off in range(1, n_cls):
        peer = (dp, lax.rem(cls + off, n_cls))
        pl.semaphore_signal(barrier, inc=1, device_id=peer, device_id_type=MESH)
    for off in range(1, n_dp):
        peer = (lax.rem(dp + off, n_dp), cls)
        pl.semaphore_signal(barrier, inc=1, device_id=peer, device_id_type=MESH)

    row8 = lax.broadcasted_iota(jnp.int32, (PAD, LANES), 0)
    slot = [slots_ref[0:1, k : k + 1] for k in range(slots)]
    count = slots_ref[0:1, slots : slots + 1]
    numbers = jnp.full((PAD, LANES), -1, jnp.int32)
    for k in range(slots):
        kept = (row8 == k) & (jnp.broadcast_to(count, row8.shape) > k)
        numbers = jnp.where(kept, jnp.broadcast_to(slot[k], row8.shape), numbers)
    ids_own[...] = numbers

    spread_from = lax.broadcasted_iota(jnp.int32, (images * n_cls, LANES), 0)
    spread_to = lax.broadcasted_iota(jnp.int32, (images * n_cls, LANES), 1)
    spread = ((spread_from // images) * PAD + spread_from % images == spread_to).astype(f32)
    labels = jnp.dot(
        jnp.broadcast_to(label_ref[...].astype(f32) + 1.0, (PAD, images * n_cls)),
        spread,
        precision=lax.Precision.HIGHEST,
        preferred_element_type=f32,
    )[0:1]

    mixed[...] = jnp.dot(att[...], w[...], preferred_element_type=f32)
    pooled_own[...] = jnp.zeros_like(pooled_own)
    rows = []
    for i in range(images):
        token = pl.ds(i * P_SIZE, P_SIZE)
        value = mixed[token] + stream[token].astype(f32)
        centred = value - jnp.mean(value, axis=1, keepdims=True)
        variance = jnp.mean(centred * centred, axis=1, keepdims=True)
        scaled = centred / jnp.sqrt(variance + NORM_EPSILON)
        rows.append(jnp.sum(scaled, axis=0, keepdims=True))
    rows.append(jnp.zeros((PAD - images, rows[0].shape[1]), f32))
    pooled = gain_ref[...] * (jnp.concatenate(rows, axis=0) * (1.0 / P_SIZE)) + shift_ref[...]
    real = lax.broadcasted_iota(jnp.int32, pooled.shape, 0) < images
    pooled = jnp.where(real, pooled, 0.0).astype(jnp.bfloat16)
    pooled_own[...] = pooled
    pooled_all[cls] = pooled

    pl.semaphore_wait(barrier, n_cls - 1 + n_dp - 1)

    def plane(off):
        return (dp, lax.rem(cls + off, n_cls))

    def pool_copy(off):
        return remote(
            pooled_own, pooled_all.at[cls], pool_s.at[off], pool_r.at[off], plane(off)
        )

    def pool_taken(off):
        source = lax.rem(cls - off + n_cls, n_cls)
        return remote(
            pooled_own, pooled_all.at[source], pool_s.at[off], pool_r.at[off], plane(off)
        )

    for off in range(1, n_cls):
        pool_copy(off).start()

    def column(off):
        chip, other = off // 2, off % 2
        return (lax.rem(z + chip, chips) * 2 + lax.rem(core + other, 2), cls)

    def ids_copy(off):
        return remote(ids_own, ids_all.at[off], ids_s.at[off], ids_r.at[off], column(off))

    order = sorted(range(1, n_dp), key=lambda off: -min(off // 2, chips - off // 2))
    for off in order:
        ids_copy(off).start()

    for k in range(slots):
        row = lax.broadcasted_iota(jnp.int32, (BLOCK_ROWS, cls_dev), 0)
        chosen = row + jnp.broadcast_to(slot[k] * BLOCK_ROWS, row.shape)
        pick = lax.broadcasted_iota(jnp.int32, row.shape, 1) == chosen
        pick = jnp.where(pick, 1.0, 0.0).astype(jnp.bfloat16)
        block = jnp.dot(pick, weight[...], preferred_element_type=f32)
        span = pl.ds(k * BLOCK_ROWS, BLOCK_ROWS)
        norm = jnp.sqrt(jnp.sum(block * block, axis=1, keepdims=True) + NORM_EPSILON)
        unit_w[span] = block / norm
        turned = block.T
        norm_row = jnp.sqrt(jnp.sum(turned * turned, axis=0, keepdims=True) + NORM_EPSILON)
        unit_wt[:, span] = turned / norm_row
        norm_w[:, span] = jnp.broadcast_to(norm_row, (PAD, BLOCK_ROWS))
    uw = split(unit_w[...])

    own_embed = jnp.dot(
        jnp.concatenate([pooled.astype(f32), jnp.zeros_like(pooled, f32)]).astype(jnp.bfloat16),
        head[...],
        preferred_element_type=f32,
    )[:PAD]
    own_norm = jnp.sqrt(jnp.sum(own_embed * own_embed, axis=1, keepdims=True) + NORM_EPSILON)
    own_unit = own_embed / own_norm

    for off in range(1, n_cls):
        pool_taken(off).wait_recv()
    group = pooled_all[...].astype(f32).reshape(n_cls * PAD, -1).astype(jnp.bfloat16)
    embedding = jnp.dot(group, head[...], preferred_element_type=f32).T
    embed_norm = jnp.sqrt(jnp.sum(embedding * embedding, axis=0, keepdims=True) + NORM_EPSILON)
    unit = split(embedding / embed_norm)

    cosine = dot3(uw, unit)
    classes, alive = [], []
    for k in range(slots):
        row = lax.broadcasted_iota(jnp.int32, (BLOCK_ROWS, LANES), 0)
        number = row + jnp.broadcast_to(slot[k] * BLOCK_ROWS, row.shape) + (cls * cls_dev + 1)
        live = jnp.broadcast_to(count, row.shape) > k
        alive.append(jnp.where(live, 1.0, 0.0))
        classes.append(jnp.where(live, number.astype(f32), -1.0))
    classes, alive = jnp.concatenate(classes, axis=0), jnp.concatenate(alive, axis=0)
    target = classes == labels
    target_cos = cosine * math.cos(ANGLE_MARGIN) - jnp.sqrt(1.0 - cosine * cosine) * math.sin(
        ANGLE_MARGIN
    )
    logits = LOGIT_SCALE * jnp.where(target, target_cos, cosine)
    exponent = jnp.where(alive > 0.0, jnp.exp(logits - LOGIT_SCALE), 0.0)
    denom_part = jnp.sum(exponent, axis=0, keepdims=True)
    target_part = jnp.sum(jnp.where(target, logits, 0.0), axis=0, keepdims=True)
    soft = jnp.where(row8 == 0, denom_part, jnp.where(row8 == 1, target_part, 0.0))
    soft_own[...] = soft
    soft_all[0] = soft

    def soft_copy(off):
        return remote(soft_own, soft_all.at[off], soft_s.at[off], soft_r.at[off], plane(off))

    for off in range(1, n_cls):
        soft_copy(off).start()
    for off in range(1, n_cls):
        soft_copy(off).wait_recv()
    total = jnp.sum(soft_all[...], axis=0)
    denominator, target_logit = total[0:1], total[1:2]

    cos_grad = LOGIT_SCALE * (exponent / denominator - jnp.where(target, 1.0, 0.0))
    cg = split(cos_grad)
    along = jnp.dot(
        jnp.ones((PAD, LANES), f32),
        (cos_grad * cosine).T,
        precision=lax.Precision.HIGHEST,
        preferred_element_type=f32,
    )[0:1]
    weight_unit_grad = dot3(unit, cg, ((1,), (1,)))
    weight_grad = (weight_unit_grad - unit_wt[...] * along) / norm_w[0:1]
    wg_own[...] = weight_grad.astype(jnp.bfloat16)
    cut = embed // n_dp

    def grad_copy(off):
        peer = column(off)
        rows_for = pl.ds(pl.multiple_of(peer[0] * cut, cut), cut)
        return remote(wg_own.at[rows_for], wg_all.at[off], wg_s.at[off], wg_r.at[off], peer)

    for off in order:
        grad_copy(off).start()

    part = dot3(split(cos_grad.T), uw)
    eg_own[...] = part.reshape(n_cls, PAD, embed)
    eg_all[0] = eg_own[cls]

    def eg_copy(off):
        peer = plane(off)
        return remote(eg_own.at[peer[1]], eg_all.at[off], eg_s.at[off], eg_r.at[off], peer)

    for off in range(1, n_cls):
        eg_copy(off).start()
    loss = jnp.log(denominator) + LOGIT_SCALE - target_logit
    lane8 = lax.broadcasted_iota(jnp.int32, (PAD, LANES), 1)
    mine = jnp.where(lane8 == row8 + cls * PAD, loss, 0.0)
    loss_ref[...] = jnp.broadcast_to(jnp.sum(mine, axis=1, keepdims=True), (PAD, LANES))
    for off in range(1, n_cls):
        eg_copy(off).wait_recv()
    unit_grad = jnp.sum(eg_all[...], axis=0)
    egrad_ref[...] = (
        unit_grad - own_unit * jnp.sum(own_unit * unit_grad, axis=1, keepdims=True)
    ) / own_norm

    sums = [jnp.zeros((cut, BLOCK_ROWS), f32) for _ in range(blocks_dev)]
    own_rows = pl.ds(pl.multiple_of(dp * cut, cut), cut)
    for off in [0] + order[::-1]:
        if off:
            ids_copy(off).wait_recv()
            grad_copy(off).wait_recv()
        for k in range(slots):
            span = pl.ds(k * BLOCK_ROWS, BLOCK_ROWS)
            if off:
                value, number = wg_all[off, :, span], ids_all[off, k : k + 1]
            else:
                value, number = wg_own[own_rows, span], ids_own[k : k + 1]
            value = value.astype(f32)
            number = jnp.broadcast_to(number, value.shape)
            for b in range(blocks_dev):
                sums[b] = sums[b] + jnp.where(number == b, value, 0.0)
    for b in range(blocks_dev):
        cgrad_ref[:, pl.ds(b * BLOCK_ROWS, BLOCK_ROWS)] = sums[b]

    for off in range(1, n_cls):
        pool_copy(off).wait_send()
        soft_copy(off).wait_send()
        eg_copy(off).wait_send()
    for off in order:
        ids_copy(off).wait_send()
        grad_copy(off).wait_send()


def per_device(
    n_dp,
    n_cls,
    attended,
    stream,
    out_proj,
    norm_gain,
    norm_shift,
    head_proj,
    class_weight,
    block_ids,
    block_count,
    labels,
):
    f32, bf16, i32 = jnp.float32, jnp.bfloat16, jnp.int32
    tokens, width = attended.shape
    images = tokens // P_SIZE
    embed = head_proj.shape[1]
    slots = block_ids.shape[2]
    columns = slots * BLOCK_ROWS
    cut = embed // n_dp
    dma = pltpu.SemaphoreType.DMA
    w, head = gather(n_dp // 2, out_proj, head_proj)
    loss, egrad, cgrad = pl.pallas_call(
        functools.partial(main_kernel, n_dp, n_cls, images),
        name="margin_softmax",
        out_shape=(
            jax.ShapeDtypeStruct((PAD, LANES), f32),
            jax.ShapeDtypeStruct((PAD, embed), f32),
            jax.ShapeDtypeStruct((cut, class_weight.shape[0]), f32),
        ),
        in_specs=[VMEM] * 9,
        out_specs=(VMEM, VMEM, VMEM),
        scratch_shapes=[
            pltpu.VMEM((tokens, width), f32),
            pltpu.VMEM((PAD, width), bf16),
            pltpu.VMEM((n_cls, PAD, width), bf16),
            pltpu.VMEM((columns, embed), f32),
            pltpu.VMEM((embed, columns), f32),
            pltpu.VMEM((PAD, columns), f32),
            pltpu.VMEM((PAD, LANES), i32),
            pltpu.VMEM((n_dp, PAD, LANES), i32),
            pltpu.VMEM((PAD, LANES), f32),
            pltpu.VMEM((n_cls, PAD, LANES), f32),
            pltpu.VMEM((n_cls, PAD, embed), f32),
            pltpu.VMEM((n_cls, PAD, embed), f32),
            pltpu.VMEM((embed, columns), bf16),
            pltpu.VMEM((n_dp, cut, columns), bf16),
            dma((n_cls,)),
            dma((n_cls,)),
            dma((n_dp,)),
            dma((n_dp,)),
            dma((n_cls,)),
            dma((n_cls,)),
            dma((n_cls,)),
            dma((n_cls,)),
            dma((n_dp,)),
            dma((n_dp,)),
        ],
        compiler_params=pltpu.CompilerParams(
            collective_id=1, has_side_effects=True, vmem_limit_bytes=32 << 20
        ),
    )(
        attended,
        stream,
        w,
        head,
        class_weight,
        norm_gain.reshape(1, width),
        norm_shift.reshape(1, width),
        jnp.concatenate([block_ids.reshape(1, slots), block_count], axis=1),
        labels.reshape(1, -1),
    )
    return loss[:images, 0], egrad[:images], cgrad.T


def solution(mesh):
    n_dp, n_cls = mesh.shape["dp"], mesh.shape["cls"]
    placed = (
        P(("dp", "cls"), None),
        P(("dp", "cls"), None),
        P("dp", None),
        P(),
        P(),
        P("dp", None),
        P("cls", None),
        P("dp", "cls", None),
        P("dp", "cls"),
        P("dp"),
    )
    return jax.shard_map(
        functools.partial(per_device, n_dp, n_cls),
        mesh=mesh,
        in_specs=placed,
        out_specs=(P(("dp", "cls")), P(("dp", "cls"), None), P("cls", "dp")),
        check_vma=False,
    )
```

time: 457 us -> 91.3 us (0.20)
  waiting for transfers between devices: 351 us -> 0 us
  Pallas kernels: 0 us -> 85.5 us
  blocking collectives: 49.8 us -> 0 us
  between operations: 15.2 us -> 1.36 us
  other arithmetic: 13.3 us -> 0.73 us
  matrix products: 12.4 us -> 0 us
  local copies, waits for them, and re-layouts: 11.9 us -> 3.48 us
    all_gather x2 -> x0, waiting for transfers between devices: 133 us -> none  [the longest x1 72.7 us: per_device(): lax.all_gather(out_proj, 'dp', axis=0, tiled=True)]
    reduce_scatter x1 -> x0, waiting for transfers between devices: 111 us -> none  [per_device(): lax.psum_scatter(dense_grad, 'dp', scatter_dimension=1, tiled=True)]
    unnamed x5 -> x0, waiting for transfers between devices: 107 us -> none
    pallas_call x0 -> x2, Pallas kernels: none -> 85.5 us  [the longest x1 43 us: gather(): pl.pallas_call(functools.partial(gather_kernel, chips), name='gather_rows...]
    psum x1 -> x0, blocking collectives: 31.2 us -> none  [per_device(): denominator, target_logit = lax.psum((denom_part, target_part), 'cls')]
    all_gather x1 -> x0, blocking collectives: 18.6 us -> none  [per_device(): group_embed = lax.all_gather(embedding, 'cls', axis=0, tiled=True)]
    dot_general x6 -> x0, matrix products: 12.4 us -> none  [the longest x1 4.19 us: per_device(): jnp.dot(columns, lax.all_gather(out_proj, 'dp', axis=0, tiled=True), pref...]
    reshape x3 -> x0, local copies, waits for them, and re-layouts: 7.91 us -> none  [the longest x2 6.2 us: per_device(): dense_grad = jnp.dot(placement, weight_grad.reshape(slot_total, -1), prec...]
  transfers between devices with their start and end apart: 4 -> 0, of which waited for: 4 -> 0; matrix products, arithmetic and copies ran while one was open for 6% -> 0% of each run, Pallas kernels for 0% -> 0%
where the time goes in v1:
time: 91.3 us; the launch traced here: 91.1 us
  Pallas kernels  85.5 us (94%)
  local copies, waits for them, and re-layouts  3.48 us (4%)
  between operations  1.36 us (1%)
    pallas_call x1, Pallas kernels, gather(): pl.pallas_call(functools.partial(gather_kernel, chips), name='gather_rows...  43 us
    pallas_call x1, Pallas kernels, per_device(): pl.pallas_call(functools.partial(main_kernel, n_dp, n_cls, images), name=...  42.5 us
    unnamed x18, local copies, waits for them, and re-layouts  2.86 us

profile of v1, /device:TPU:1, one launch (start us, length us, event | category | flops | bytes accessed | tf_op | source)
XLA Modules:
  0.0 91.1 jit_solution(5855192267296975885)
XLA Ops:
  1.3 0.7 pad_add_fusion.slots_ref
  2.0 0.0 copy-start.6
  2.0 0.8 copy-done.6
  2.8 0.0 copy-start.7
  2.8 0.8 copy-done.7
  3.6 0.0 copy-start
  3.6 0.0 copy-start.1
  3.6 0.0 copy-start.2
  3.6 0.0 copy-start.3
  3.6 0.0 copy-start.4
  3.6 0.0 copy-start.5
  3.6 43.0 %gather_rows.1 = (bf16[1024,1024]{1,0:T(8,128)(2,1)S(1)}, bf16[1024,512]{1,0:T(8,128)(2,1)S(1)}) custom-call(bf16[32,1024]{1,0:T(8,128)(2,1)S(1)} %copy-done.6, bf16[32,512]{1,0:T(8,128)(2,1)S(1)} %copy-done.7), custom_call_target="tpu_custom_call" | custom-call | flops 40000000000 | bytes 20971520 | tf_op jit(solution)/shard_map/gather_rows/pallas_call | solution.py:147
  46.6 0.0 copy-done
  46.6 0.0 copy-done.1
  46.6 0.0 copy-done.2
  46.6 0.0 copy-done.3
  46.7 0.0 copy-done.4
  46.7 0.0 copy-done.5
  46.7 42.5 %margin_softmax.1 = (f32[8,128]{1,0:T(8,128)S(1)}, f32[8,512]{1,0:T(8,128)S(1)}, f32[16,1024]{1,0:T(8,128)S(1)}) custom-call(bf16[864,1024]{1,0:T(8,128)(2,1)S(1)} %copy-done, bf16[864,1024]{1,0:T(8,128)(2,1)S(1)} %copy-done.1, bf16[1024,1024]{1,0:T(8,128)(2,1)S(1)} %get-tuple-element.8.w, bf16[1024,512]{1,0:T(8,128)(2,1)S(1)} %get-tuple-element.9.head, ...), custom_call_target="tpu_custom_call" | custom-call | tf_op jit(solution)/shard_map/margin_softmax/pallas_call | solution.py:451
  89.2 0.6 slice_reduce_fusion
  89.8 0.6 copy.16
  90.4 0.6 copy.17
Async XLA Ops:
  2.0 0.8 copy-start.6
  2.8 0.8 copy-start.7
  3.6 43.0 %copy-start = (bf16[864,1024]{1,0:T(8,128)(2,1)S(1)}, bf16[864,1024]{1,0:T(8,128)(2,1)}, u32[]{:S(2)}) copy-start(bf16[864,1024]{1,0:T(8,128)(2,1)} %att.1) | copy-start | bytes 5308420
  3.6 43.0 %copy-start.1 = (bf16[864,1024]{1,0:T(8,128)(2,1)S(1)}, bf16[864,1024]{1,0:T(8,128)(2,1)}, u32[]{:S(2)}) copy-start(bf16[864,1024]{1,0:T(8,128)(2,1)} %stream.1) | copy-start | bytes 5308420
  3.6 43.0 %copy-start.2 = (bf16[1024,512]{1,0:T(8,128)(2,1)S(1)}, bf16[1024,512]{1,0:T(8,128)(2,1)}, u32[]{:S(2)}) copy-start(bf16[1024,512]{1,0:T(8,128)(2,1)} %weight.1) | copy-start | bytes 3145732
  3.6 43.0 %copy-start.3 = (f32[1024]{0:T(1024)S(1)}, f32[1024]{0:T(1024)}, u32[]{:S(2)}) copy-start(f32[1024]{0:T(1024)} %param.13) | copy-start | bytes 12292
  3.6 43.0 %copy-start.4 = (f32[1024]{0:T(1024)S(1)}, f32[1024]{0:T(1024)}, u32[]{:S(2)}) copy-start(f32[1024]{0:T(1024)} %param.14) | copy-start | bytes 12292
  3.6 43.0 %copy-start.5 = (s32[96]{0:T(128)S(1)}, s32[96]{0:T(128)}, u32[]{:S(2)}) copy-start(s32[96]{0:T(128)} %param.19) | copy-start | bytes 1156

commit v2 on v1

v2 whole, which is shorter than its diff:
```python
import functools
import math

import jax
import jax.numpy as jnp
from jax import lax
from jax.experimental import pallas as pl
from jax.experimental.pallas import tpu as pltpu
from jax.sharding import PartitionSpec as P

P_SIZE = 144
BLOCK_ROWS = 128
LOGIT_SCALE = 64.0
ANGLE_MARGIN = 0.5
NORM_EPSILON = 1e-06
LANES = 128
PAD = 8

MESH = pl.DeviceIdType.MESH
VMEM = pl.BlockSpec(memory_space=pltpu.VMEM)
SMEM = pl.BlockSpec(memory_space=pltpu.SMEM)
HBM = pl.BlockSpec(memory_space=pltpu.HBM)


def remote(src, dst, send, recv, device):
    return pltpu.make_async_remote_copy(
        src_ref=src,
        dst_ref=dst,
        send_sem=send,
        recv_sem=recv,
        device_id=device,
        device_id_type=MESH,
    )


def split(x):
    high = x.astype(jnp.bfloat16)
    low = (x - high.astype(jnp.float32)).astype(jnp.bfloat16)
    return high, low


def dot3(a, b, contract=((1,), (0,))):
    (ah, al), (bh, bl) = a, b
    dims = (contract, ((), ()))
    mul = functools.partial(
        lax.dot_general, dimension_numbers=dims, preferred_element_type=jnp.float32
    )
    return mul(ah, bh) + (mul(ah, bl) + mul(al, bh))


SIDE = 4
LEAPS = (6, -6, 3, -3)
RELAY = 4


def gather_kernel(chips, op_ref, hp_ref, wh_ref, own_sem, line_s, line_r, plane_s, plane_r, sib_s, sib_r):
    dp, cls = lax.axis_index("dp"), lax.axis_index("cls")
    z, core = dp // 2, dp % 2
    x, y = cls % SIDE, cls // SIDE
    shard, total = op_ref.shape[0], wh_ref.shape[1]
    width = op_ref.shape[1]
    half, wide = shard // 2, total // 2
    colour = (x + 2 * y) % SIDE
    sibling = (z * 2 + 1 - core, cls)

    def along(off):
        return (((z + off + chips) % chips) * 2 + core, cls)

    plane = [
        (dp, y * SIDE + (x + 1) % SIDE),
        (dp, y * SIDE + (x + SIDE - 1) % SIDE),
        (dp, ((y + 1) % SIDE) * SIDE + x),
        (dp, ((y + SIDE - 1) % SIDE) * SIDE + x),
    ]
    mine = pl.ds(pl.multiple_of(dp * shard, shard), shard)
    own = [
        pltpu.make_async_copy(op_ref, wh_ref.at[mine, pl.ds(0, width)], own_sem.at[0]),
        pltpu.make_async_copy(hp_ref, wh_ref.at[mine, pl.ds(width, total - width)], own_sem.at[1]),
    ]
    for copy in own:
        copy.start()
    barrier = pltpu.get_barrier_semaphore()
    line = [along(off) for off in (1, -1, 2, -2, *LEAPS)]
    for peer in (*line, sibling, *plane):
        pl.semaphore_signal(barrier, inc=1, device_id=peer, device_id_type=MESH)
    pl.semaphore_wait(barrier, len(line) + 5)
    for copy in own:
        copy.wait()

    def quarter(off, part=None):
        chip = (z - off + chips) % chips
        start = pl.multiple_of((chip * 2 + core) * shard + (colour // 2) * half, half)
        column = (colour % 2) * wide
        size = wide if part is None else wide // 2
        if part is not None:
            column = column + part * size
        return wh_ref.at[pl.ds(start, half), pl.ds(pl.multiple_of(column, LANES), size)]

    def count(rows, send, recv):
        block = wh_ref.at[pl.ds(0, rows)]
        return remote(block, block, send, recv, sibling)

    def pass_on(off, step):
        block = quarter(off)
        return remote(block, block, line_s, line_r.at[(off + step) % chips], along(step))

    def spread(off):
        block, arrived = quarter(off), plane_r.at[off % chips]
        for peer in plane[:2]:
            remote(block, block, plane_s, arrived, peer).start()
        for part, peer in enumerate(plane[2:]):
            piece = quarter(off, part)
            remote(piece, piece, plane_s, arrived, peer).start()

    def hand(off):
        start = pl.multiple_of(((z - off + chips) % chips * 2 + core) * shard, shard)
        block = wh_ref.at[pl.ds(start, shard)]
        remote(block, block, sib_s, sib_r, sibling).start()

    row_q = half // 2

    def taken(*offs):
        for off in offs:
            pass_on(off, 0).wait_recv()
            if off in LEAPS:
                pass_on(off, 1).start()
                pass_on(off, -1).start()
            if off == LEAPS[0]:
                pass_on(off, 2).start()
            spread(off)

    def complete(*offs):
        for off in offs:
            count(3 * row_q, plane_s, plane_r.at[off % chips]).wait_recv()
            hand(off)

    for step in (*LEAPS, 1, -1):
        pass_on(0, step).start()
    hand(0)
    taken(1, -1)
    taken(3, -3)
    complete(1, -1)
    taken(6, -6)
    complete(3, -3)
    taken(2, -2, 4, -4)
    complete(6, -6)
    taken(5, -5, 7, -7, 8)
    complete(2, -2, 4, -4)
    complete(5, -5, 7, -7, 8)
    others = chips - 1
    count(chips * shard, sib_s, sib_r).wait_recv()
    count(others * row_q, line_s, line_r.at[0]).wait_send()
    count(others * 3 * row_q, plane_s, plane_r.at[0]).wait_send()
    count(chips * shard, sib_s, sib_r).wait_send()


def gather(chips, out_proj, head_proj):
    shard, width = out_proj.shape
    embed = head_proj.shape[1]
    dma = pltpu.SemaphoreType.DMA
    return pl.pallas_call(
        functools.partial(gather_kernel, chips),
        name="gather_rows",
        out_shape=jax.ShapeDtypeStruct((2 * chips * shard, width + embed), out_proj.dtype),
        in_specs=[HBM, HBM],
        out_specs=VMEM,
        scratch_shapes=[dma((2,)), dma, dma((chips,)), dma, dma((chips,)), dma, dma],
        compiler_params=pltpu.CompilerParams(
            collective_id=0, has_side_effects=True, vmem_limit_bytes=4 << 20
        ),
        cost_estimate=pl.CostEstimate(
            flops=40_000_000_000, bytes_accessed=20 << 20, transcendentals=0
        ),
    )(out_proj, head_proj)


def main_kernel(
    n_dp,
    n_cls,
    images,
    att,
    stream,
    wh_ref,
    weight,
    gain_ref,
    shift_ref,
    ids_ref,
    count_ref,
    label_ref,
    loss_ref,
    egrad_ref,
    cgrad_ref,
    mixed,
    pooled_own,
    pooled_all,
    unit_w,
    unit_wt,
    norm_w,
    ids_own,
    ids_all,
    soft_own,
    soft_all,
    eg_own,
    eg_all,
    wg_own,
    wg_all,
    pool_s,
    pool_r,
    ids_s,
    ids_r,
    soft_s,
    soft_r,
    eg_s,
    eg_r,
    wg_s,
    wg_r,
    far_own,
    far_all,
    far_s,
    far_r,
):
    f32 = jnp.float32
    dp, cls = lax.axis_index("dp"), lax.axis_index("cls")
    chips = n_dp // 2
    z, core = dp // 2, dp % 2
    slots = ids_ref.shape[1]
    width = att.shape[1]
    embed = wh_ref.shape[1] - width
    columns = slots * BLOCK_ROWS
    cls_dev = weight.shape[0]
    blocks_dev = cls_dev // BLOCK_ROWS

    barrier = pltpu.get_barrier_semaphore()
    for off in range(1, n_cls):
        peer = (dp, lax.rem(cls + off, n_cls))
        pl.semaphore_signal(barrier, inc=1, device_id=peer, device_id_type=MESH)
    for off in range(1, n_dp):
        peer = (lax.rem(dp + off, n_dp), cls)
        pl.semaphore_signal(barrier, inc=1, device_id=peer, device_id_type=MESH)

    row8 = lax.broadcasted_iota(jnp.int32, (PAD, LANES), 0)
    slot = [ids_ref[0:1, k : k + 1] for k in range(slots)]
    count = jnp.full((1, LANES), count_ref[0, 0], jnp.int32)
    numbers = jnp.full((PAD, LANES), -1, jnp.int32)
    for k in range(slots):
        kept = (row8 == k) & (jnp.broadcast_to(count, row8.shape) > k)
        numbers = jnp.where(kept, jnp.broadcast_to(slot[k], row8.shape), numbers)
    ids_own[...] = numbers

    spread_from = lax.broadcasted_iota(jnp.int32, (images * n_cls, LANES), 0)
    spread_to = lax.broadcasted_iota(jnp.int32, (images * n_cls, LANES), 1)
    spread = ((spread_from // images) * PAD + spread_from % images == spread_to).astype(f32)
    labels = jnp.dot(
        jnp.broadcast_to(label_ref[...].astype(f32) + 1.0, (PAD, images * n_cls)),
        spread,
        precision=lax.Precision.HIGHEST,
        preferred_element_type=f32,
    )[0:1]

    mixed[...] = jnp.dot(att[...], wh_ref[:, :width], preferred_element_type=f32)
    pooled_own[...] = jnp.zeros_like(pooled_own)
    rows = []
    for i in range(images):
        token = pl.ds(i * P_SIZE, P_SIZE)
        value = mixed[token] + stream[token].astype(f32)
        centred = value - jnp.mean(value, axis=1, keepdims=True)
        variance = jnp.mean(centred * centred, axis=1, keepdims=True)
        scaled = centred / jnp.sqrt(variance + NORM_EPSILON)
        rows.append(jnp.sum(scaled, axis=0, keepdims=True))
    rows.append(jnp.zeros((PAD - images, rows[0].shape[1]), f32))
    pooled = gain_ref[...] * (jnp.concatenate(rows, axis=0) * (1.0 / P_SIZE)) + shift_ref[...]
    real = lax.broadcasted_iota(jnp.int32, pooled.shape, 0) < images
    pooled = jnp.where(real, pooled, 0.0).astype(jnp.bfloat16)
    pooled_own[...] = pooled
    pooled_all[cls] = pooled

    pl.semaphore_wait(barrier, n_cls - 1 + n_dp - 1)

    def plane(off):
        return (dp, lax.rem(cls + off, n_cls))

    def pool_copy(off):
        return remote(
            pooled_own, pooled_all.at[cls], pool_s, pool_r, plane(off)
        )

    def tally(ref, send, recv):
        block = ref.at[pl.ds(1, ref.shape[0] - 1)]
        return remote(block, block, send, recv, plane(1))

    for off in range(1, n_cls):
        pool_copy(off).start()

    def column(shift, other):
        return (((z + shift + chips) % chips) * 2 + (core + other) % 2, cls)

    near = [(s, o) for s in range(1 - RELAY, RELAY + 1) for o in (0, 1) if s or o]

    def ids_copy(shift, other):
        held = ids_all.at[2 * (shift % chips) + other]
        return remote(ids_own, held, ids_s, ids_r, column(shift, other))

    for shift, other in near:
        ids_copy(shift, other).start()

    for k in range(slots):
        row = lax.broadcasted_iota(jnp.int32, (BLOCK_ROWS, cls_dev), 0)
        chosen = row + jnp.broadcast_to(slot[k] * BLOCK_ROWS, row.shape)
        pick = lax.broadcasted_iota(jnp.int32, row.shape, 1) == chosen
        pick = jnp.where(pick, 1.0, 0.0).astype(jnp.bfloat16)
        block = jnp.dot(pick, weight[...], preferred_element_type=f32)
        span = pl.ds(k * BLOCK_ROWS, BLOCK_ROWS)
        norm = jnp.sqrt(jnp.sum(block * block, axis=1, keepdims=True) + NORM_EPSILON)
        unit_w[span] = block / norm
        turned = block.T
        norm_row = jnp.sqrt(jnp.sum(turned * turned, axis=0, keepdims=True) + NORM_EPSILON)
        unit_wt[:, span] = turned / norm_row
        norm_w[:, span] = jnp.broadcast_to(norm_row, (PAD, BLOCK_ROWS))
    uw = split(unit_w[...])

    head = wh_ref[:, width:]
    own_embed = jnp.dot(
        jnp.concatenate([pooled.astype(f32), jnp.zeros_like(pooled, f32)]).astype(jnp.bfloat16),
        head,
        preferred_element_type=f32,
    )[:PAD]
    own_norm = jnp.sqrt(jnp.sum(own_embed * own_embed, axis=1, keepdims=True) + NORM_EPSILON)
    own_unit = own_embed / own_norm

    tally(pooled_all, pool_s, pool_r).wait_recv()
    group = pooled_all[...].astype(f32).reshape(n_cls * PAD, -1).astype(jnp.bfloat16)
    embedding = jnp.dot(group, head, preferred_element_type=f32).T
    embed_norm = jnp.sqrt(jnp.sum(embedding * embedding, axis=0, keepdims=True) + NORM_EPSILON)
    unit = split(embedding / embed_norm)

    cosine = dot3(uw, unit)
    classes, alive = [], []
    for k in range(slots):
        row = lax.broadcasted_iota(jnp.int32, (BLOCK_ROWS, LANES), 0)
        number = row + jnp.broadcast_to(slot[k] * BLOCK_ROWS, row.shape) + (cls * cls_dev + 1)
        live = jnp.broadcast_to(count, row.shape) > k
        alive.append(jnp.where(live, 1.0, 0.0))
        classes.append(jnp.where(live, number.astype(f32), -1.0))
    classes, alive = jnp.concatenate(classes, axis=0), jnp.concatenate(alive, axis=0)
    target = classes == labels
    target_cos = cosine * math.cos(ANGLE_MARGIN) - jnp.sqrt(1.0 - cosine * cosine) * math.sin(
        ANGLE_MARGIN
    )
    logits = LOGIT_SCALE * jnp.where(target, target_cos, cosine)
    exponent = jnp.where(alive > 0.0, jnp.exp(logits - LOGIT_SCALE), 0.0)
    denom_part = jnp.sum(exponent, axis=0, keepdims=True)
    target_part = jnp.sum(jnp.where(target, logits, 0.0), axis=0, keepdims=True)
    soft = jnp.where(row8 == 0, denom_part, jnp.where(row8 == 1, target_part, 0.0))
    soft_own[...] = soft
    soft_all[0] = soft

    def soft_copy(off):
        return remote(soft_own, soft_all.at[off], soft_s, soft_r, plane(off))

    for off in range(1, n_cls):
        soft_copy(off).start()
    tally(soft_all, soft_s, soft_r).wait_recv()
    total = jnp.sum(soft_all[...], axis=0)
    denominator, target_logit = total[0:1], total[1:2]

    cos_grad = LOGIT_SCALE * (exponent / denominator - jnp.where(target, 1.0, 0.0))
    cg = split(cos_grad)
    along = jnp.dot(
        jnp.ones((PAD, LANES), f32),
        (cos_grad * cosine).T,
        precision=lax.Precision.HIGHEST,
        preferred_element_type=f32,
    )[0:1]
    weight_unit_grad = dot3(unit, cg, ((1,), (1,)))
    weight_grad = (weight_unit_grad - unit_wt[...] * along) / norm_w[0:1]
    wg_own[...] = weight_grad.astype(jnp.bfloat16)
    cut = embed // n_dp

    legs = [(s, o, RELAY) for s in range(RELAY, -1, -1) for o in (0, 1) if s or o]
    legs += [(-s, o, -RELAY) for s in range(RELAY - 1, -1, -1) for o in (0, 1) if s or o]
    legs += [(w * s, o, 0) for s in range(RELAY - 1, 0, -1) for w in (1, -1) for o in (0, 1)]
    legs += [(0, 1, 0)]

    def columns_of(chip, at):
        return pl.ds(pl.multiple_of((((chip + 2 * chips) % chips) * 2 + at) * cut, cut), cut)

    def leg_copy(t):
        shift, other, onward = legs[t]
        rows_for = columns_of(z + shift + onward, (core + other) % 2)
        return remote(wg_own.at[rows_for], wg_all.at[t], wg_s, wg_r.at[t], column(shift, other))

    for t in range(len(legs)):
        leg_copy(t).start()

    part = dot3(split(cos_grad.T), uw)
    eg_own[...] = part.reshape(n_cls, PAD, embed)
    eg_all[0] = eg_own[cls]

    def eg_copy(off):
        peer = plane(off)
        return remote(eg_own.at[peer[1]], eg_all.at[off], eg_s, eg_r, peer)

    for off in range(1, n_cls):
        eg_copy(off).start()
    loss = jnp.log(denominator) + LOGIT_SCALE - target_logit
    lane8 = lax.broadcasted_iota(jnp.int32, (PAD, LANES), 1)
    mine = jnp.where(lane8 == row8 + cls * PAD, loss, 0.0)
    loss_ref[...] = jnp.broadcast_to(jnp.sum(mine, axis=1, keepdims=True), (PAD, LANES))
    ids_got = ids_all.at[pl.ds(0, len(near))]
    remote(ids_got, ids_got, ids_s, ids_r, plane(1)).wait_recv()

    def add(sums, value, numbers):
        for k in range(slots):
            part = value[:, k * BLOCK_ROWS : (k + 1) * BLOCK_ROWS].astype(f32)
            number = jnp.broadcast_to(numbers[k : k + 1], part.shape)
            sums = [s + jnp.where(number == b, part, 0.0) for b, s in enumerate(sums)]
        return sums

    def gathered(onward):
        rows_for = columns_of(z + onward, core)
        sums = [jnp.zeros((cut, BLOCK_ROWS), f32) for _ in range(blocks_dev)]
        sums = add(sums, wg_own[rows_for], ids_own[...])
        for t in reversed(range(len(legs))):
            shift, other, onto = legs[t]
            if onto == onward:
                leg_copy(t).wait_recv()
                sums = add(sums, wg_all[t], ids_all[2 * (shift % chips) + other])
        return sums

    def relay_copy(way):
        to = column((-RELAY, RELAY)[way], 0)
        return remote(far_own.at[way], far_all.at[way], far_s, far_r.at[way], to)

    for way in (0, 1):
        for b, part in enumerate(gathered((-RELAY, RELAY)[way])):
            far_own[way, :, pl.ds(b * BLOCK_ROWS, BLOCK_ROWS)] = part.astype(jnp.bfloat16)
        relay_copy(way).start()

    tally(eg_all, eg_s, eg_r).wait_recv()
    unit_grad = jnp.sum(eg_all[...], axis=0)
    egrad_ref[...] = (
        unit_grad - own_unit * jnp.sum(own_unit * unit_grad, axis=1, keepdims=True)
    ) / own_norm

    sums = gathered(0)
    for way in (0, 1):
        relay_copy(way).wait_recv()
        sums = [
            s + far_all[way, :, pl.ds(b * BLOCK_ROWS, BLOCK_ROWS)].astype(f32)
            for b, s in enumerate(sums)
        ]
    for b in range(blocks_dev):
        cgrad_ref[:, pl.ds(b * BLOCK_ROWS, BLOCK_ROWS)] = sums[b]

    tally(pooled_all, pool_s, pool_r).wait_send()
    tally(soft_all, soft_s, soft_r).wait_send()
    tally(eg_all, eg_s, eg_r).wait_send()
    remote(ids_got, ids_got, ids_s, ids_r, plane(1)).wait_send()
    legs_sent = wg_all.at[pl.ds(0, len(legs))]
    remote(legs_sent, legs_sent, wg_s, wg_r.at[0], plane(1)).wait_send()
    remote(far_all, far_all, far_s, far_r.at[0], plane(1)).wait_send()


def per_device(
    n_dp,
    n_cls,
    attended,
    stream,
    out_proj,
    norm_gain,
    norm_shift,
    head_proj,
    class_weight,
    block_ids,
    block_count,
    labels,
):
    f32, bf16, i32 = jnp.float32, jnp.bfloat16, jnp.int32
    tokens, width = attended.shape
    images = tokens // P_SIZE
    embed = head_proj.shape[1]
    slots = block_ids.shape[2]
    columns = slots * BLOCK_ROWS
    cut = embed // n_dp
    dma = pltpu.SemaphoreType.DMA
    projections = gather(n_dp // 2, out_proj, head_proj)
    loss, egrad, cgrad = pl.pallas_call(
        functools.partial(main_kernel, n_dp, n_cls, images),
        name="margin_softmax",
        out_shape=(
            jax.ShapeDtypeStruct((PAD, LANES), f32),
            jax.ShapeDtypeStruct((PAD, embed), f32),
            jax.ShapeDtypeStruct((cut, class_weight.shape[0]), f32),
        ),
        in_specs=[VMEM] * 7 + [SMEM, VMEM],
        out_specs=(VMEM, VMEM, VMEM),
        scratch_shapes=[
            pltpu.VMEM((tokens, width), f32),
            pltpu.VMEM((PAD, width), bf16),
            pltpu.VMEM((n_cls, PAD, width), bf16),
            pltpu.VMEM((columns, embed), f32),
            pltpu.VMEM((embed, columns), f32),
            pltpu.VMEM((PAD, columns), f32),
            pltpu.VMEM((PAD, LANES), i32),
            pltpu.VMEM((n_dp, PAD, LANES), i32),
            pltpu.VMEM((PAD, LANES), f32),
            pltpu.VMEM((n_cls, PAD, LANES), f32),
            pltpu.VMEM((n_cls, PAD, embed), f32),
            pltpu.VMEM((n_cls, PAD, embed), f32),
            pltpu.VMEM((embed, columns), bf16),
            pltpu.VMEM((n_dp, cut, columns), bf16),
            *([dma] * 9),
            dma((n_dp,)),
            pltpu.VMEM((2, cut, class_weight.shape[0]), bf16),
            pltpu.VMEM((2, cut, class_weight.shape[0]), bf16),
            dma,
            dma((2,)),
        ],
        compiler_params=pltpu.CompilerParams(
            collective_id=1, has_side_effects=True, vmem_limit_bytes=32 << 20
        ),
    )(
        attended,
        stream,
        projections,
        class_weight,
        norm_gain.reshape(1, width),
        norm_shift.reshape(1, width),
        block_ids.reshape(1, slots),
        block_count,
        labels.reshape(1, -1),
    )
    return loss[:images, 0], egrad[:images], cgrad.T


def solution(mesh):
    n_dp, n_cls = mesh.shape["dp"], mesh.shape["cls"]
    placed = (
        P(("dp", "cls"), None),
        P(("dp", "cls"), None),
        P("dp", None),
        P(),
        P(),
        P("dp", None),
        P("cls", None),
        P("dp", "cls", None),
        P("dp", "cls"),
        P("dp"),
    )
    return jax.shard_map(
        functools.partial(per_device, n_dp, n_cls),
        mesh=mesh,
        in_specs=placed,
        out_specs=(P(("dp", "cls")), P(("dp", "cls"), None), P("cls", "dp")),
        check_vma=False,
    )
```

time: 91.3 us -> 77.4 us (0.85)
  Pallas kernels: 85.5 us -> 72.3 us
    pallas_call x1, Pallas kernels: 42.5 us -> 34.6 us  [per_device(): pl.pallas_call(functools.partial(main_kernel, n_dp, n_cls, images), name=...]
    pallas_call x1, Pallas kernels: 43 us -> 37.7 us  [gather(): pl.pallas_call(functools.partial(gather_kernel, chips), name='gather_rows...]
    unnamed x18 -> x20, local copies, waits for them, and re-layouts: 2.86 us -> 2.85 us
where the time goes in v2:
time: 77.4 us; the launch traced here: 77.1 us
  Pallas kernels  72.3 us (93%)
  local copies, waits for them, and re-layouts  3.48 us (4%)
  between operations  1.39 us (2%)
    pallas_call x1, Pallas kernels, gather(): pl.pallas_call(functools.partial(gather_kernel, chips), name='gather_rows...  37.7 us
    pallas_call x1, Pallas kernels, per_device(): pl.pallas_call(functools.partial(main_kernel, n_dp, n_cls, images), name=...  34.6 us
    unnamed x20, local copies, waits for them, and re-layouts  2.85 us

profile of v2, /device:TPU:1, one launch (start us, length us, event | category | flops | bytes accessed | tf_op | source)
XLA Modules:
  0.0 77.1 jit_solution(2629566478849359617)
XLA Ops:
  1.3 0.0 copy-start.7
  1.3 0.8 %copy-done.7 = bf16[32,1024]{1,0:T(8,128)(2,1)S(1)} copy-done((bf16[32,1024]{1,0:T(8,128)(2,1)S(1)}, bf16[32,1024]{1,0:T(8,128)(2,1)}, u32[]{:S(2)}) %copy-start.7) | copy-done | bytes 65560
  2.1 0.0 copy-start.8
  2.1 0.8 copy-done.8
  2.9 0.0 copy-start
  2.9 0.0 copy-start.1
  2.9 0.0 copy-start.2
  2.9 0.0 copy-start.3
  2.9 0.0 copy-start.4
  2.9 0.0 copy-start.5
  2.9 0.0 copy-start.6
  2.9 37.7 %gather_rows.1.wh_ref = bf16[1024,1536]{1,0:T(8,128)(2,1)S(1)} custom-call(bf16[32,1024]{1,0:T(8,128)(2,1)S(1)} %copy-done.7, bf16[32,512]{1,0:T(8,128)(2,1)S(1)} %copy-done.8), custom_call_target="tpu_custom_call" | custom-call | flops 40000000000 | bytes 20971520 | tf_op jit(solution)/shard_map/gather_rows/pallas_call | solution.py:161
  40.6 0.0 copy-done
  40.6 0.0 copy-done.1
  40.7 0.0 copy-done.2
  40.7 0.0 copy-done.3
  40.7 0.0 copy-done.4
  40.7 0.0 copy-done.5
  40.7 0.0 copy-done.6
  40.7 34.6 %margin_softmax.1 = (f32[8,128]{1,0:T(8,128)S(1)}, f32[8,512]{1,0:T(8,128)S(1)}, f32[16,1024]{1,0:T(8,128)S(1)}) custom-call(bf16[864,1024]{1,0:T(8,128)(2,1)S(1)} %copy-done, bf16[864,1024]{1,0:T(8,128)(2,1)S(1)} %copy-done.1, bf16[1024,1536]{1,0:T(8,128)(2,1)S(1)} %gather_rows.1.wh_ref, bf16[1024,512]{1,0:T(8,128)(2,1)S(1)} %copy-done.2, ...), custom_call_target="tpu_custom_call" | custom-call | tf_op jit(solution)/shard_map/margin_softmax/pallas_call | solution.py:487
  75.3 0.6 slice_reduce_fusion
  75.9 0.6 copy.16
  76.5 0.6 copy.17
Async XLA Ops:
  1.3 0.8 %copy-start.7 = (bf16[32,1024]{1,0:T(8,128)(2,1)S(1)}, bf16[32,1024]{1,0:T(8,128)(2,1)}, u32[]{:S(2)}) copy-start(bf16[32,1024]{1,0:T(8,128)(2,1)} %op_ref.1) | copy-start | bytes 196612
  2.1 0.8 copy-start.8
  2.9 37.8 %copy-start = (bf16[864,1024]{1,0:T(8,128)(2,1)S(1)}, bf16[864,1024]{1,0:T(8,128)(2,1)}, u32[]{:S(2)}) copy-start(bf16[864,1024]{1,0:T(8,128)(2,1)} %att.1) | copy-start | bytes 5308420
  2.9 37.8 %copy-start.1 = (bf16[864,1024]{1,0:T(8,128)(2,1)S(1)}, bf16[864,1024]{1,0:T(8,128)(2,1)}, u32[]{:S(2)}) copy-start(bf16[864,1024]{1,0:T(8,128)(2,1)} %stream.1) | copy-start | bytes 5308420
  2.9 37.8 %copy-start.2 = (bf16[1024,512]{1,0:T(8,128)(2,1)S(1)}, bf16[1024,512]{1,0:T(8,128)(2,1)}, u32[]{:S(2)}) copy-start(bf16[1024,512]{1,0:T(8,128)(2,1)} %weight.1) | copy-start | bytes 3145732
  2.9 37.8 %copy-start.3 = (f32[1024]{0:T(1024)S(1)}, f32[1024]{0:T(1024)}, u32[]{:S(2)}) copy-start(f32[1024]{0:T(1024)} %param.13) | copy-start | bytes 12292
  2.9 37.8 %copy-start.4 = (f32[1024]{0:T(1024)S(1)}, f32[1024]{0:T(1024)}, u32[]{:S(2)}) copy-start(f32[1024]{0:T(1024)} %param.14) | copy-start | bytes 12292
  2.9 37.8 %copy-start.5 = (s32[1,1,3]{2,1,0:T(1,128)S(1)}, s32[1,1,3]{2,1,0:T(1,128)}, u32[]{:S(2)}) copy-start(s32[1,1,3]{2,1,0:T(1,128)} %param.17) | copy-start | bytes 40
  2.9 37.8 %copy-start.6 = (s32[96]{0:T(128)S(1)}, s32[96]{0:T(128)}, u32[]{:S(2)}) copy-start(s32[96]{0:T(128)} %param.19) | copy-start | bytes 1156
